TPU v7x, 512 devices: a whole 4x4x16 slice. The times are simulated.
512 devices in a mesh: ctx: 32 (over z, y_lo), exp: 8 (over x, core), dp: 2 (over y_hi).
Axes of the slice: x: 4, y: 4 (y_hi: 2, y_lo: 2; y = y_hi * 2 + y_lo), z: 16, core: 2. Of those that a mesh axis runs over, the one named last changes fastest.
Arguments:
- hidden_in: bfloat16 [2, 32768, 1024], P('dp', ('ctx', 'exp')), may hold values from -6 to 6
- queries: bfloat16 [2, 32768, 1024], P('dp', ('ctx', 'exp')), may hold values from -6 to 6
- keys: bfloat16 [2, 32768, 1024], P('dp', ('ctx', 'exp')), may hold values from -6 to 6
- values: bfloat16 [2, 32768, 1024], P('dp', ('ctx', 'exp')), may hold values from -6 to 6
- log_decay: float32 [2, 32768, 8], P('dp', ('ctx', 'exp')), may hold values from -1 to 0
- retention_gain: float32 [1024], replicated, may hold values from 0.25 to 1.75
- norm_gain: float32 [1024], replicated, may hold values from 0.25 to 1.75
- routes: int32 [2, 32768, 2], P('dp', ('ctx', 'exp')), may hold values from 0 to 63, all different within a row; in each aligned block of 128 rows (0 to 127, 128 to 255, ..., all dimensions but the last counted through in order) at most 5 rows name the same one
- route_weights: float32 [2, 32768, 2], P('dp', ('ctx', 'exp')), may hold values from 0.1 to 1
- w_gate: bfloat16 [64, 1024, 1408], P(('ctx', 'dp'), 'exp'), may hold values from -0.1875 to 0.1875
- w_up: bfloat16 [64, 1024, 1408], P(('ctx', 'dp'), 'exp'), may hold values from -0.1875 to 0.1875
- w_down: bfloat16 [64, 1024, 1408], P(('ctx', 'dp'), 'exp'), may hold values from -0.15625 to 0.15625
Outputs:
- output: bfloat16 [2, 32768, 1024], P('dp', ('ctx', 'exp'))
Inputs may be any that keep to these rules, and one draw needn't show every extreme that they name: `routes`: in each aligned block of 128 positions (the positions of one device) no expert is named more than 5 times, and a position's 2 experts differ.
All inputs are finite; a program needn't handle non-finite values.
Results may differ from a plain program's by a relative error of at most 0.007.
Values may be sent and summed in bfloat16 or wider, within the bound.
No kernel may reach another device: no remote copies, remote signals or barrier semaphores. Data moves between devices by JAX's collectives and lax.ppermute only.
A program may use at most 128 MiB of HBM per device.

v0:
```python
import jax
import jax.numpy as jnp
from jax import lax
from jax.sharding import Mesh, PartitionSpec as P

CTX = ("z", "ylo")
EXP = ("x", "core")
OWNERS = ("z", "ylo", "yhi")


def exchange(blocks, axes):
    return lax.all_to_all(blocks, axes, split_axis=0, concat_axis=0, tiled=True)


def rotate(vectors, token_position):
    half_dim = vectors.shape[-1] // 2
    inverse = 10000.0 ** (-jnp.arange(half_dim, dtype=jnp.float32) / half_dim)
    angles = token_position.astype(jnp.float32)[:, None] * inverse[None, :]
    cosine = jnp.cos(angles)[:, None, :]
    sine_part = jnp.sin(angles)[:, None, :]
    leading = vectors[..., :half_dim]
    trailing = vectors[..., half_dim:]
    return jnp.concatenate(
        [leading * cosine - trailing * sine_part, trailing * cosine + leading * sine_part], axis=-1
    )


def entering_state(block_summary, block_log):
    member_count = lax.axis_size(EXP)
    ctx_count = lax.axis_size(CTX)
    own_head = lax.axis_index(EXP)
    own_ctx = lax.axis_index(CTX)
    all_logs = lax.all_gather(block_log, CTX + EXP, axis=0).reshape(ctx_count, member_count, -1)
    head_logs = lax.dynamic_index_in_dim(all_logs, own_head, 2, keepdims=False)
    group_logs = jnp.sum(head_logs, axis=1)
    own_logs = lax.dynamic_index_in_dim(head_logs, own_ctx, 0, keepdims=False)
    members = jnp.arange(member_count)
    ctxs = jnp.arange(ctx_count)
    summaries = exchange(block_summary.astype(jnp.bfloat16), EXP).astype(jnp.float32)
    after = jnp.exp(
        jnp.sum(jnp.where(members[None, :] > members[:, None], own_logs[None, :], 0.0), 1)
    )
    group_sum = jnp.sum(after[:, None, None] * summaries, axis=0)
    group_sums = lax.all_gather(group_sum.astype(jnp.bfloat16), CTX, axis=0).astype(jnp.float32)
    between = (ctxs[None, :] > ctxs[:, None]) & (ctxs[None, :] < own_ctx)
    reach = jnp.exp(jnp.sum(jnp.where(between, group_logs[None, :], 0.0), 1))
    reach = jnp.where(ctxs < own_ctx, reach, 0.0)
    leading = jnp.sum(reach[:, None, None] * group_sums, axis=0)
    to_block = jnp.exp(
        jnp.sum(jnp.where(members[None, :] < members[:, None], own_logs[None, :], 0.0), 1)
    )
    inner = (members[None, None, :] > members[None, :, None]) & (
        members[None, None, :] < members[:, None, None]
    )
    inner = jnp.exp(jnp.sum(jnp.where(inner, own_logs[None, None, :], 0.0), 2))
    inner = jnp.where(members[None, :] < members[:, None], inner, 0.0)
    entering = to_block[:, None, None] * leading[None] + jnp.sum(
        inner[:, :, None, None] * summaries[None], axis=1
    )
    return exchange(entering.astype(jnp.bfloat16), EXP)


def body(
    hidden_in,
    queries,
    keys,
    values,
    log_decay,
    retention_gain,
    norm_gain,
    routes,
    route_weights,
    w_gate,
    w_up,
    w_down,
):
    tok_rows = hidden_in.shape[1]
    model_width = hidden_in.shape[2]
    head_count = log_decay.shape[2]
    head_dim = model_width // head_count
    block_index = lax.axis_index(CTX) * lax.axis_size(EXP) + lax.axis_index(EXP)
    token_position = block_index * tok_rows + jnp.arange(tok_rows, dtype=jnp.int32)
    per_head_keys = rotate(
        keys[0].astype(jnp.float32).reshape(tok_rows, head_count, head_dim), token_position
    ).astype(jnp.bfloat16)
    per_head_values = values[0].reshape(tok_rows, head_count, head_dim)
    running_total = jnp.cumsum(log_decay[0], axis=0)
    trailing_decay = jnp.exp(running_total[-1][None, :] - running_total)
    block_summary = jnp.einsum(
        "qpf,qpy->pfy",
        per_head_keys.astype(jnp.float32) * trailing_decay[:, :, None],
        per_head_values.astype(jnp.float32),
        precision=lax.Precision.HIGHEST,
    )
    state_in = entering_state(block_summary, running_total[-1])
    per_head_queries = (
        rotate(
            queries[0].astype(jnp.float32).reshape(tok_rows, head_count, head_dim), token_position
        )
        * head_dim ** (-0.5)
    ).astype(jnp.bfloat16)
    scores = jnp.einsum(
        "thd,shd->hts", per_head_queries, per_head_keys, preferred_element_type=jnp.float32
    )
    causal = jnp.arange(tok_rows)[:, None] >= jnp.arange(tok_rows)[None, :]
    spread = running_total.T[:, :, None] - running_total.T[:, None, :]
    weights = jnp.where(
        causal[None], scores * jnp.exp(jnp.where(causal[None], spread, 0.0)), 0.0
    ).astype(jnp.bfloat16)
    inside = jnp.einsum(
        "hts,shd->thd", weights, per_head_values, preferred_element_type=jnp.float32
    )
    external_part = jnp.exp(running_total)[:, :, None] * jnp.einsum(
        "wjc,jco->wjo", per_head_queries, state_in, preferred_element_type=jnp.float32
    )
    retrieved = inside + external_part
    centre = jnp.mean(retrieved, axis=-1, keepdims=True)
    deviation = retrieved - centre
    variance = jnp.mean(deviation * deviation, axis=-1, keepdims=True)
    normalized = (deviation * lax.rsqrt(variance + 1e-05)).reshape(tok_rows, model_width)
    residual = hidden_in[0].astype(jnp.float32) + retention_gain * normalized
    square_mean = jnp.mean(residual * residual, axis=-1, keepdims=True)
    normed = (residual * lax.rsqrt(square_mean + 1e-06) * norm_gain).astype(jnp.bfloat16)
    expert_count = lax.axis_size(OWNERS)
    top_count = routes.shape[2]
    capacity = (tok_rows * top_count * 5 + 4 * expert_count - 1) // (4 * expert_count)
    slot_count = expert_count * capacity
    route_rows = routes[0]
    expert_hits = (
        route_rows.reshape(tok_rows * top_count)[:, None]
        == jnp.arange(expert_count, dtype=jnp.int32)[None, :]
    ).astype(jnp.int32)
    earlier = jnp.cumsum(expert_hits, axis=0) - expert_hits
    slot_rank = jnp.sum(earlier * expert_hits, axis=1).reshape(tok_rows, top_count)
    destination = route_rows * capacity + slot_rank
    slot_lanes = jnp.arange(slot_count, dtype=jnp.int32)
    placing = jnp.any(destination[None, :, :] == slot_lanes[:, None, None], axis=2).astype(
        jnp.bfloat16
    )
    outgoing = jnp.dot(placing, normed, preferred_element_type=jnp.float32).astype(jnp.bfloat16)
    lanes = 128
    packed = (expert_count, capacity * model_width // lanes, lanes)
    arrived = exchange(outgoing.reshape(packed), OWNERS).reshape(slot_count, model_width)
    gate_full = lax.all_gather(w_gate[0], EXP, axis=0, tiled=True)
    up_full = lax.all_gather(w_up[0], EXP, axis=0, tiled=True)
    down_full = lax.all_gather(w_down[0], EXP, axis=0, tiled=True)
    gate_next = jnp.dot(arrived, gate_full, preferred_element_type=jnp.float32)
    up_next = jnp.dot(arrived, up_full, preferred_element_type=jnp.float32)
    hidden = (jax.nn.silu(gate_next) * up_next).astype(jnp.bfloat16)
    expert_out = lax.dot_general(
        hidden, down_full, (((1,), (1,)), ((), ())), preferred_element_type=jnp.float32
    ).astype(jnp.bfloat16)
    returned = exchange(expert_out.reshape(packed), OWNERS).reshape(slot_count, model_width)
    output = residual
    for route_index in range(top_count):
        picking = (destination[:, route_index][:, None] == slot_lanes[None, :]).astype(jnp.bfloat16)
        routed = jnp.dot(picking, returned, preferred_element_type=jnp.float32)
        output = output + route_weights[0][:, route_index][:, None] * routed
    return output.astype(jnp.bfloat16)[None]


def solution(mesh):
    ctx, exp, dp = (mesh.shape["ctx"], mesh.shape["exp"], mesh.shape["dp"])
    split = Mesh(
        mesh.devices.reshape(ctx // 2, 2, exp // 2, 2, dp), ("z", "ylo", "x", "core", "yhi")
    )
    tokens = P("yhi", CTX + EXP, None)
    experts = P(OWNERS, EXP, None)
    in_specs = (tokens,) * 5 + (P(), P()) + (tokens,) * 2 + (experts,) * 3
    return jax.shard_map(body, mesh=split, in_specs=in_specs, out_specs=tokens, check_vma=False)
```

profile of v0, /device:TPU:8, one launch (start us, length us, event | category | flops | bytes accessed | tf_op | source)
XLA Modules:
  0.0 633.6 jit_solution(9688745371011176003)
XLA Ops:
  6.6 1.2 copy.84
  7.8 0.2 copy.108
  8.0 0.2 copy.109
  8.2 0.2 copy.87
  8.4 0.2 copy.110
  8.7 0.2 copy.111
  9.0 0.2 reduce_window_sum.26
  9.2 1.0 copy.114
  10.2 0.3 multiply_cosine_fusion
  10.6 0.3 multiply_subtract_fusion
  10.9 0.7 copy-done.1
  11.7 1.5 convolution_convert_fusion.1
  13.2 4.3 all-to-all-start
  17.6 305.4 %all-gather.4 = f32[256,1,8]{2,1,0:T(1,128)S(1)} all-gather(f32[1,1,8]{2,1,0:T(1,128)S(1)} %get-tuple-element.21), channel_id=1, replica_groups=mesh['z'=16,'ylo'=2,'x'=4,'core'=2,'yhi'=2] {'z','ylo','x','core'}, dimensions={0}, use_global_device_ids=true | all-gather | bytes 8224 | tf_op jit(solution)/shard_map/all_gather | solution.py:33
  323.2 0.1 select_reduce_fusion.3
  323.3 0.7 multiply_reduce_fusion.3
  324.1 0.7 all-gather.12.cloned.1.call-update
  324.9 0.7 all-gather.14.cloned.1.call-update
  325.6 0.5 all-gather.16.cloned.1.call-update
  326.2 0.5 dynamic-slice_reduce_fusion
  327.3 0.6 reduce-window.6
  327.9 0.2 slice_reduce_fusion.2
  328.6 0.6 multiply_reduce_fusion
  329.2 0.2 copy.100
  329.4 125.0 %all-gather.10.cloned.1.call-done = bf16[4096,128]{1,0:T(8,128)(2,1)} async-done(((bf16[128,128]{1,0:T(8,128)(2,1)}), bf16[4096,128]{1,0:T(8,128)(2,1)}) %all-gather.10.cloned.1.call-update) | async-done | bytes 1048592 | tf_op jit(solution)/shard_map/all_gather | solution.py:44
  454.4 1.5 fusion.8
  456.0 0.8 add_convert_fusion
  456.9 4.2 all-to-all-start.1
  461.2 0.2 fusion.22
  461.4 7.1 %all-to-all-done.1 = bf16[8,128,128]{1,2,0:T(8,128)(2,1)S(1)} async-done(((bf16[8,128,128]{1,2,0:T(8,128)(2,1)}), bf16[8,128,128]{1,2,0:T(8,128)(2,1)S(1)}, u32[]{:S(2)}, u32[]{:S(2)}) %all-to-all-start.1) | async-done | bytes 262176 | tf_op jit(solution)/shard_map/all_to_all | solution.py:12
  468.6 0.3 fusion.13
  468.9 0.6 fusion.53
  469.7 0.2 copy.101
  469.9 0.2 multiply_reduce_fusion.1
  470.2 0.4 convolution_convert_fusion
  470.6 0.3 reshape.252
  470.9 52.5 %all_to_all.20 = bf16[64,40,128]{2,1,0:T(8,128)(2,1)S(1)} all-to-all(bf16[64,40,128]{2,1,0:T(8,128)(2,1)S(1)} %reshape.252), channel_id=1, replica_groups=mesh['z'=16,'ylo'=2,'x'=4,'core'=2,'yhi'=2] {'z','ylo','yhi'}, dimensions={0} | all-to-all | bytes 1310720 | tf_op jit(solution)/shard_map/all_to_all | solution.py:12
  523.4 0.3 reshape.253
  523.7 4.3 fusion.3
  528.0 36.3 %all-gather.16.cloned.1.call-done = bf16[1,1024,1408]{2,1,0:T(8,128)(2,1)} async-done(((bf16[1,128,1408]{2,1,0:T(8,128)(2,1)}), bf16[1,1024,1408]{2,1,0:T(8,128)(2,1)}) %all-gather.16.cloned.1.call-update) | async-done | bytes 2883600 | tf_op jit(solution)/shard_map/all_gather | solution.py:146
  564.3 5.4 fusion.9
  569.8 1.1 reshape.254
  570.9 15.7 %all-to-all-start.3 = ((bf16[64,40,128]{2,1,0:T(8,128)(2,1)}), bf16[64,40,128]{2,1,0:T(8,128)(2,1)S(1)}, u32[]{:S(2)}, u32[]{:S(2)}) async-start(bf16[64,40,128]{2,1,0:T(8,128)(2,1)} %reshape.254), calls=%async_computation.3 | async-start | bytes 1310720 | tf_op jit(solution)/shard_map/all_to_all | solution.py:12
  586.8 0.2 slice_reduce_fusion
  587.0 38.4 %all-to-all-done.3 = bf16[64,40,128]{2,1,0:T(8,128)(2,1)S(1)} async-done(((bf16[64,40,128]{2,1,0:T(8,128)(2,1)}), bf16[64,40,128]{2,1,0:T(8,128)(2,1)S(1)}, u32[]{:S(2)}, u32[]{:S(2)}) %all-to-all-start.3) | async-done | bytes 655392 | tf_op jit(solution)/shard_map/all_to_all | solution.py:12
  625.4 0.3 reshape.255
  625.7 0.4 fusion.16
  626.0 1.1 fusion.19
  (71 shorter events, 2.5 us)
Async XLA Ops:
  6.5 1.7 copy-start.5
  8.0 0.9 copy-start.8
  10.9 0.7 copy-start.1
  10.9 0.8 copy-start.3
  10.9 315.8 %copy-start.9 = (s32[1,128,2]{1,2,0:T(2,128)S(1)}, s32[1,128,2]{1,2,0:T(2,128)}, u32[]{:S(2)}) copy-start(s32[1,128,2]{1,2,0:T(2,128)} %param.19) | copy-start | bytes 3076
  13.2 310.1 %all-to-all-start = ((bf16[8,128,128]{2,1,0:T(8,128)(2,1)}), bf16[8,128,128]{2,1,0:T(8,128)(2,1)S(1)}, u32[]{:S(2)}, u32[]{:S(2)}) async-start(bf16[8,128,128]{2,1,0:T(8,128)(2,1)} %convolution_convert_fusion.1), calls=%async_computation | async-start | bytes 524288 | tf_op jit(solution)/shard_map/all_to_all | solution.py:12
  17.5 436.9 %all-gather.10.cloned.1.call-start = ((), (), s32[]{:S(2)}) async-start(), calls=%async_computation.4 | async-start | bytes 1081344 | tf_op jit(solution)/shard_map/all_gather | solution.py:44
  324.1 199.6 %all-gather.12.cloned.1.call-start = ((), (), s32[]{:S(2)}) async-start(), calls=%async_computation.5 | async-start | bytes 3244032 | tf_op jit(solution)/shard_map/all_gather | solution.py:144
  324.8 203.2 %all-gather.14.cloned.1.call-start = ((), (), s32[]{:S(2)}) async-start(), calls=%async_computation.6 | async-start | bytes 3244032 | tf_op jit(solution)/shard_map/all_gather | solution.py:145
  325.6 238.7 %all-gather.16.cloned.1.call-start = ((), (), s32[]{:S(2)}) async-start(), calls=%async_computation.7 | async-start | bytes 3244032 | tf_op jit(solution)/shard_map/all_gather | solution.py:146
  455.9 12.9 %copy-start.2 = (bf16[128,8,64]{2,0,1:T(8,128)(2,1)S(1)}, bf16[128,8,64]{2,0,1:T(8,128)(2,1)}, u32[]{:S(2)}) copy-start(bf16[128,8,64]{2,0,1:T(8,128)(2,1)} %copy-done.1) | copy-start | bytes 393220
  455.9 12.9 %copy-start.4 = (bf16[128,8,64]{2,0,1:T(8,128)(2,1)S(1)}, bf16[128,8,64]{2,0,1:T(8,128)(2,1)}, u32[]{:S(2)}) copy-start(bf16[128,8,64]{2,0,1:T(8,128)(2,1)} %copy-done.3) | copy-start | bytes 393220
  456.9 11.7 %all-to-all-start.1 = ((bf16[8,128,128]{1,2,0:T(8,128)(2,1)}), bf16[8,128,128]{1,2,0:T(8,128)(2,1)S(1)}, u32[]{:S(2)}, u32[]{:S(2)}) async-start(bf16[8,128,128]{1,2,0:T(8,128)(2,1)} %add_convert_fusion), calls=%async_computation.1 | async-start | bytes 524288 | tf_op jit(solution)/shard_map/all_to_all | solution.py:12
  468.9 1.0 copy-start
  468.9 1.0 copy-start.6
  469.5 0.7 copy-start.7
  569.8 17.2 %copy-start.10 = (f32[1,128,2]{1,2,0:T(2,128)S(1)}, f32[1,128,2]{1,2,0:T(2,128)}, u32[]{:S(2)}) copy-start(f32[1,128,2]{1,2,0:T(2,128)} %param.20) | copy-start | bytes 3076
  570.9 54.5 %all-to-all-start.3 = ((bf16[64,40,128]{2,1,0:T(8,128)(2,1)}), bf16[64,40,128]{2,1,0:T(8,128)(2,1)S(1)}, u32[]{:S(2)}, u32[]{:S(2)}) async-start(bf16[64,40,128]{2,1,0:T(8,128)(2,1)} %reshape.254), calls=%async_computation.3 | async-start | bytes 1310720 | tf_op jit(solution)/shard_map/all_to_all | solution.py:12
Sparse Core Ops, SparseCore 0:
  324.2 130.1 all-gather.9
  456.5 34.1 all-gather.11
  492.9 34.6 all-gather.13
  529.6 34.6 all-gather.15
where the time goes:
time: 634 us
  blocking collectives  358 us (56%)
  waiting for transfers between devices  209 us (33%)
  starting transfers between devices  24.4 us (4%)
  matrix products  14 us (2%)
  between operations  13.6 us (2%)
  local copies, waits for them, and re-layouts  8.17 us (1%)
  other arithmetic  6.77 us (1%)
    all_gather x1, blocking collectives, entering_state(): lax.all_gather(block_log, CTX + EXP, axis=0)  305 us
    all_gather x1, waiting for transfers between devices, entering_state(): lax.all_gather(group_sum.astype(jnp.bfloat16), CTX, axis=0)  125 us
    all_to_all x1, blocking collectives, exchange(): return lax.all_to_all(blocks, axes, split_axis=0, concat_axis=0, tiled=True)  52.5 us
    all_to_all x3, waiting for transfers between devices, exchange(): return lax.all_to_all(blocks, axes, split_axis=0, concat_axis=0, tiled=True)  45.5 us
    all_gather x1, waiting for transfers between devices, body(): down_full = lax.all_gather(w_down[0], EXP, axis=0, tiled=True)  36.3 us
    all_to_all x3, starting transfers between devices, exchange(): return lax.all_to_all(blocks, axes, split_axis=0, concat_axis=0, tiled=True)  24.2 us
  transfers between devices with their start and end apart: 7, of which 4 were waited for; matrix products, arithmetic and copies ran while one was open for 2% of the time, Pallas kernels for 0%

commit v1 on v0

--- a/solution.py
+++ b/solution.py
@@ -143,7 +143,9 @@
     arrived = exchange(outgoing.reshape(packed), OWNERS).reshape(slot_count, model_width)
     gate_full = lax.all_gather(w_gate[0], EXP, axis=0, tiled=True)
     up_full = lax.all_gather(w_up[0], EXP, axis=0, tiled=True)
-    down_full = lax.all_gather(w_down[0], EXP, axis=0, tiled=True)
+    down_full = jnp.concatenate(
+        lax.all_to_all(jnp.stack([w_down[0]] * lax.axis_size(EXP)), EXP, 0, 0), axis=0
+    )
     gate_next = jnp.dot(arrived, gate_full, preferred_element_type=jnp.float32)
     up_next = jnp.dot(arrived, up_full, preferred_element_type=jnp.float32)
     hidden = (jax.nn.silu(gate_next) * up_next).astype(jnp.bfloat16)

time: 634 us -> 629 us (level)
  blocking collectives: 358 us -> 305 us
  waiting for transfers between devices: 209 us -> 239 us
  starting transfers between devices: 24.4 us -> 34.5 us
    all_to_all x1 -> x0, blocking collectives: 52.5 us -> none  [exchange(): return lax.all_to_all(blocks, axes, split_axis=0, concat_axis=0, tiled=True)]
    all_to_all x3 -> x4, waiting for transfers between devices: 45.5 us -> 83.3 us  [exchange(): return lax.all_to_all(blocks, axes, split_axis=0, concat_axis=0, tiled=True)]
    all_gather x1 -> x0, waiting for transfers between devices: 36.3 us -> none  [body(): down_full = lax.all_gather(w_down[0], EXP, axis=0, tiled=True)]
    all_to_all x0 -> x1, waiting for transfers between devices: none -> 28.7 us  [body(): lax.all_to_all(jnp.stack([w_down[0]] * lax.axis_size(EXP)), EXP, 0, 0)]
    all_to_all x3 -> x4, starting transfers between devices: 24.2 us -> 30.5 us  [exchange(): return lax.all_to_all(blocks, axes, split_axis=0, concat_axis=0, tiled=True)]
  transfers between devices with their start and end apart: 7 -> 8, of which waited for: 4 -> 5; matrix products, arithmetic and copies ran while one was open for 2% -> 3% of each run, Pallas kernels for 0% -> 0%
where the time goes in v1:
time: 629 us; the launch traced here: 628 us
  blocking collectives  305 us (48%)
  waiting for transfers between devices  239 us (38%)
  starting transfers between devices  34.5 us (5%)
  local copies, waits for them, and re-layouts  14.4 us (2%)
  matrix products  14.3 us (2%)
  between operations  13.6 us (2%)
  other arithmetic  7.36 us (1%)
    all_gather x1, blocking collectives, entering_state(): lax.all_gather(block_log, CTX + EXP, axis=0)  305 us
    all_gather x1, waiting for transfers between devices, entering_state(): lax.all_gather(group_sum.astype(jnp.bfloat16), CTX, axis=0)  125 us
    all_to_all x4, waiting for transfers between devices, exchange(): return lax.all_to_all(blocks, axes, split_axis=0, concat_axis=0, tiled=True)  83.3 us
    all_to_all x4, starting transfers between devices, exchange(): return lax.all_to_all(blocks, axes, split_axis=0, concat_axis=0, tiled=True)  30.5 us
    all_to_all x1, waiting for transfers between devices, body(): lax.all_to_all(jnp.stack([w_down[0]] * lax.axis_size(EXP)), EXP, 0, 0)  28.7 us
  transfers between devices with their start and end apart: 8, of which 5 were waited for; matrix products, arithmetic and copies ran while one was open for 3% of the time, Pallas kernels for 0%

profile of v1, /device:TPU:8, one launch (start us, length us, event | category | flops | bytes accessed | tf_op | source)
XLA Modules:
  0.0 628.4 jit_solution(12841282803206582759)
XLA Ops:
  6.6 1.2 copy.84
  7.8 0.2 copy.108
  8.0 0.2 copy.109
  8.4 0.2 copy.110
  8.6 0.2 copy.111
  9.1 0.6 fusion.48
  9.8 1.0 copy.114
  10.9 0.3 multiply_cosine_fusion
  11.2 0.3 multiply_subtract_fusion
  11.5 0.7 copy-done.3
  12.3 1.5 convolution_convert_fusion.2
  13.8 4.3 all-to-all-start
  18.2 305.4 %all-gather.3 = f32[256,1,8]{2,1,0:T(1,128)S(1)} all-gather(f32[1,1,8]{2,1,0:T(1,128)S(1)} %get-tuple-element.21), channel_id=1, replica_groups=mesh['z'=16,'ylo'=2,'x'=4,'core'=2,'yhi'=2] {'z','ylo','x','core'}, dimensions={0}, use_global_device_ids=true | all-gather | bytes 8224 | tf_op jit(solution)/shard_map/all_gather | solution.py:33
  323.9 0.7 multiply_reduce_fusion.3
  324.7 0.7 all-gather.10.cloned.1.call-update
  325.9 0.9 copy.94
  326.9 0.6 reduce-window.6
  327.5 0.2 slice_reduce_fusion.2
  328.0 0.5 dynamic-slice_reduce_fusion
  328.9 0.6 multiply_reduce_fusion
  329.5 0.2 copy.100
  329.7 125.3 %all-gather.8.cloned.1.call-done = bf16[4096,128]{1,0:T(8,128)(2,1)} async-done(((bf16[128,128]{1,0:T(8,128)(2,1)}), bf16[4096,128]{1,0:T(8,128)(2,1)}) %all-gather.8.cloned.1.call-update) | async-done | bytes 1048592 | tf_op jit(solution)/shard_map/all_gather | solution.py:44
  455.0 1.5 fusion.6
  456.6 0.8 add_convert_fusion
  457.5 4.2 all-to-all-start.1
  461.7 0.2 fusion.18
  461.9 7.2 %all-to-all-done.1 = bf16[8,128,128]{1,2,0:T(8,128)(2,1)S(1)} async-done(((bf16[8,128,128]{1,2,0:T(8,128)(2,1)}), bf16[8,128,128]{1,2,0:T(8,128)(2,1)S(1)}, u32[]{:S(2)}, u32[]{:S(2)}) %all-to-all-start.1) | async-done | bytes 262176 | tf_op jit(solution)/shard_map/all_to_all | solution.py:12
  469.1 0.3 fusion.8
  469.5 0.6 fusion.49
  470.2 0.2 copy.101
  470.6 0.4 convolution_convert_fusion
  471.1 1.1 reshape.256
  472.2 14.4 %all-to-all-start.2 = ((bf16[64,40,128]{2,1,0:T(8,128)(2,1)}), bf16[64,40,128]{2,1,0:T(8,128)(2,1)S(1)}, u32[]{:S(2)}, u32[]{:S(2)}) async-start(bf16[64,40,128]{2,1,0:T(8,128)(2,1)} %reshape.256), calls=%async_computation.2 | async-start | bytes 1310720 | tf_op jit(solution)/shard_map/all_to_all | solution.py:12
  486.6 0.7 all-gather.12.cloned.1.call-update
  487.3 37.6 %all-to-all-done.2 = bf16[64,40,128]{2,1,0:T(8,128)(2,1)S(1)} async-done(((bf16[64,40,128]{2,1,0:T(8,128)(2,1)}), bf16[64,40,128]{2,1,0:T(8,128)(2,1)S(1)}, u32[]{:S(2)}, u32[]{:S(2)}) %all-to-all-start.2) | async-done | bytes 655392 | tf_op jit(solution)/shard_map/all_to_all | solution.py:12
  524.9 1.8 stack.3
  526.7 3.8 all-to-all-start.3
  530.5 2.1 reshape.257
  532.6 4.5 fusion.1
  537.1 28.7 %all-to-all-done.3 = bf16[8,128,1408]{2,1,0:T(8,128)(2,1)S(1)} async-done(((bf16[8,128,1408]{2,1,0:T(8,128)(2,1)}), bf16[8,128,1408]{2,1,0:T(8,128)(2,1)S(1)}, u32[]{:S(2)}, u32[]{:S(2)}) %all-to-all-start.3) | async-done | bytes 2883616 | tf_op jit(solution)/shard_map/all_to_all | solution.py:147
  565.8 5.6 convolution_convert_fusion.1
  571.4 2.2 reshape.259
  573.6 7.7 %all-to-all-start.4 = ((bf16[64,40,128]{2,1,0:T(8,128)(2,1)}), bf16[64,40,128]{2,1,0:T(8,128)(2,1)S(1)}, u32[]{:S(2)}, u32[]{:S(2)}) async-start(bf16[64,40,128]{2,1,0:T(8,128)(2,1)} %reshape.259), calls=%async_computation.4 | async-start | bytes 1310720 | tf_op jit(solution)/shard_map/all_to_all | solution.py:12
  581.5 0.2 slice_reduce_fusion
  581.7 38.5 %all-to-all-done.4 = bf16[64,40,128]{2,1,0:T(8,128)(2,1)S(1)} async-done(((bf16[64,40,128]{2,1,0:T(8,128)(2,1)}), bf16[64,40,128]{2,1,0:T(8,128)(2,1)S(1)}, u32[]{:S(2)}, u32[]{:S(2)}) %all-to-all-start.4) | async-done | bytes 655392 | tf_op jit(solution)/shard_map/all_to_all | solution.py:12
  620.1 0.3 reshape.260
  620.4 0.4 fusion.11
  620.8 1.1 fusion.14
  (78 shorter events, 2.9 us)
Async XLA Ops:
  6.5 1.7 copy-start.8
  7.7 1.1 copy-start.11
  11.2 314.3 %copy-start.12 = (s32[1,128,2]{1,2,0:T(2,128)S(1)}, s32[1,128,2]{1,2,0:T(2,128)}, u32[]{:S(2)}) copy-start(s32[1,128,2]{1,2,0:T(2,128)} %param.19) | copy-start | bytes 3076
  11.5 0.7 copy-start.3
  11.5 0.8 copy-start.5
  13.8 310.1 %all-to-all-start = ((bf16[8,128,128]{2,1,0:T(8,128)(2,1)}), bf16[8,128,128]{2,1,0:T(8,128)(2,1)S(1)}, u32[]{:S(2)}, u32[]{:S(2)}) async-start(bf16[8,128,128]{2,1,0:T(8,128)(2,1)} %convolution_convert_fusion.2), calls=%async_computation | async-start | bytes 524288 | tf_op jit(solution)/shard_map/all_to_all | solution.py:12
  18.1 436.9 %all-gather.8.cloned.1.call-start = ((), (), s32[]{:S(2)}) async-start(), calls=%async_computation.5 | async-start | bytes 1081344 | tf_op jit(solution)/shard_map/all_gather | solution.py:44
  324.7 207.9 %all-gather.10.cloned.1.call-start = ((), (), s32[]{:S(2)}) async-start(), calls=%async_computation.6 | async-start | bytes 3244032 | tf_op jit(solution)/shard_map/all_gather | solution.py:144
  329.5 140.0 %copy-start.4 = (bf16[128,8,64]{2,0,1:T(8,128)(2,1)S(1)}, bf16[128,8,64]{2,0,1:T(8,128)(2,1)}, u32[]{:S(2)}) copy-start(bf16[128,8,64]{2,0,1:T(8,128)(2,1)} %copy-done.3) | copy-start | bytes 393220
  329.5 140.0 %copy-start.6 = (bf16[128,8,64]{2,0,1:T(8,128)(2,1)S(1)}, bf16[128,8,64]{2,0,1:T(8,128)(2,1)}, u32[]{:S(2)}) copy-start(bf16[128,8,64]{2,0,1:T(8,128)(2,1)} %copy-done.5) | copy-start | bytes 393220
  457.5 11.7 %all-to-all-start.1 = ((bf16[8,128,128]{1,2,0:T(8,128)(2,1)}), bf16[8,128,128]{1,2,0:T(8,128)(2,1)S(1)}, u32[]{:S(2)}, u32[]{:S(2)}) async-start(bf16[8,128,128]{1,2,0:T(8,128)(2,1)} %add_convert_fusion), calls=%async_computation.1 | async-start | bytes 524288 | tf_op jit(solution)/shard_map/all_to_all | solution.py:12
  461.9 8.6 %copy-start.1 = (bf16[1,128,1024]{2,1,0:T(8,128)(2,1)S(1)}, bf16[1,128,1024]{2,1,0:T(8,128)(2,1)}, u32[]{:S(2)}) copy-start(bf16[1,128,1024]{2,1,0:T(8,128)(2,1)} %param.12) | copy-start | bytes 786436
  461.9 8.6 %copy-start.9 = (f32[1024]{0:T(1024)S(1)}, f32[1024]{0:T(1024)}, u32[]{:S(2)}) copy-start(f32[1024]{0:T(1024)} %param.17) | copy-start | bytes 12292
  469.5 1.2 copy-start.10
  470.4 54.4 %copy-start.7 = (bf16[1,128,1408]{2,1,0:T(8,128)(2,1)S(1)}, bf16[1,128,1408]{2,1,0:T(8,128)(2,1)}, u32[]{:S(2)}) copy-start(bf16[1,128,1408]{2,1,0:T(8,128)(2,1)} %param.23) | copy-start | bytes 1081348
  472.2 52.7 %all-to-all-start.2 = ((bf16[64,40,128]{2,1,0:T(8,128)(2,1)}), bf16[64,40,128]{2,1,0:T(8,128)(2,1)S(1)}, u32[]{:S(2)}, u32[]{:S(2)}) async-start(bf16[64,40,128]{2,1,0:T(8,128)(2,1)} %reshape.256), calls=%async_computation.2 | async-start | bytes 1310720 | tf_op jit(solution)/shard_map/all_to_all | solution.py:12
  486.5 79.3 %all-gather.12.cloned.1.call-start = ((), (), s32[]{:S(2)}) async-start(), calls=%async_computation.7 | async-start | bytes 3244032 | tf_op jit(solution)/shard_map/all_gather | solution.py:145
  524.9 1.8 copy-start
  526.7 39.2 %all-to-all-start.3 = ((bf16[8,128,1408]{2,1,0:T(8,128)(2,1)}), bf16[8,128,1408]{2,1,0:T(8,128)(2,1)S(1)}, u32[]{:S(2)}, u32[]{:S(2)}) async-start(bf16[8,128,1408]{2,1,0:T(8,128)(2,1)} %stack.3), calls=%async_computation.3 | async-start | bytes 5767168 | tf_op jit(solution)/shard_map/all_to_all | solution.py:147
  571.4 10.2 %copy-start.13 = (f32[1,128,2]{1,2,0:T(2,128)S(1)}, f32[1,128,2]{1,2,0:T(2,128)}, u32[]{:S(2)}) copy-start(f32[1,128,2]{1,2,0:T(2,128)} %param.20) | copy-start | bytes 3076
  571.4 49.0 %copy-start.2 = (bf16[1,128,1024]{2,1,0:T(8,128)(2,1)S(1)}, bf16[1,128,1024]{2,1,0:T(8,128)(2,1)}, u32[]{:S(2)}) copy-start(bf16[1,128,1024]{2,1,0:T(8,128)(2,1)} %param.12) | copy-start | bytes 786436
  573.6 46.5 %all-to-all-start.4 = ((bf16[64,40,128]{2,1,0:T(8,128)(2,1)}), bf16[64,40,128]{2,1,0:T(8,128)(2,1)S(1)}, u32[]{:S(2)}, u32[]{:S(2)}) async-start(bf16[64,40,128]{2,1,0:T(8,128)(2,1)} %reshape.259), calls=%async_computation.4 | async-start | bytes 1310720 | tf_op jit(solution)/shard_map/all_to_all | solution.py:12
Sparse Core Ops, SparseCore 0:
  324.8 130.1 all-gather.7
  457.1 34.1 all-gather.9
  493.5 34.6 all-gather.11
